TPU v7x, 128 devices: a whole 4x4x4 slice. The times are simulated.
128 devices in a mesh: gx: 16 (over z_lo, x, core), gy: 8 (over y, z_hi).
Axes of the slice: x: 4, y: 4, z: 4 (z_hi: 2, z_lo: 2; z = z_hi * 2 + z_lo), core: 2. Of those that a mesh axis runs over, the one named last changes fastest.
Arguments:
- features: bfloat16 [64, 128, 64, 128], P(None, 'gx', 'gy'), may hold values from -6 to 6
- cotangent: bfloat16 [64, 128, 64, 128], P(None, 'gx', 'gy'), may hold values from -6 to 6
- block_mask: int32 [16, 8, 16], P('gx', 'gy'), may hold values from 0 to 1, as said below
- kernel_one: bfloat16 [3, 3, 3, 64, 64], replicated, may hold values from -0.15625 to 0.15625
- kernel_two: bfloat16 [3, 3, 3, 64, 64], replicated, may hold values from -0.15625 to 0.15625
Outputs:
- grad_features: bfloat16 [64, 128, 64, 128], P(None, 'gx', 'gy')
- grad_one: float32 [3, 3, 3, 64, 64], replicated
- grad_two: float32 [3, 3, 3, 64, 64], replicated
Inputs may be any that keep to these rules, and one draw needn't show every extreme that they name: `block_mask`: 1 marks an active block of 8 x 8 x 8 cells, 0 an empty one.
All inputs are finite; a program needn't handle non-finite values.
Results may differ from a plain program's by a relative error of at most 0.0032.
Values may be sent and summed in bfloat16 or wider, within the bound.
No kernel may reach another device: no remote copies, remote signals or barrier semaphores. Data moves between devices by JAX's collectives and lax.ppermute only.
A program may use at most 192 MiB of HBM per device.

v0:
```python
import math
import jax
import jax.numpy as jnp
from jax import lax
from jax.sharding import PartitionSpec as P

BS = 8


def padded_2(cells, sides, width):
    for axis, dim in sides:
        count = lax.axis_size(axis)
        ends = count - 1
        head = lax.slice_in_dim(cells, 0, width, axis=dim)
        tail = lax.slice_in_dim(cells, cells.shape[dim] - width, cells.shape[dim], axis=dim)
        cells = jnp.concatenate(
            [
                lax.ppermute(tail, axis, [(i, (i + 1) % count) for i in range(ends)]),
                cells,
                lax.ppermute(head, axis, [((i + 1) % count, i) for i in range(ends)]),
            ],
            axis=dim,
        )
    return cells


def upsample(block_mask):
    nbx, nby, nbz = block_mask.shape
    wide = jnp.broadcast_to(block_mask[:, None, :, None, :, None], (nbx, BS, nby, BS, nbz, BS))
    return wide.reshape(nbx * BS, nby * BS, nbz * BS)


def flip_kernel(kernel):
    return jnp.transpose(jnp.flip(kernel, (0, 1, 2)), (0, 1, 2, 4, 3))


def silu_slope(value):
    sig = jax.nn.sigmoid(value)
    return sig * (1.0 + value * (1.0 - sig))


def stack_depth(source):
    depth = source.shape[-1]
    padded = jnp.pad(source, ((0, 0), (0, 0), (0, 0), (1, 1)))
    return jnp.concatenate(
        [padded[..., 0:depth], padded[..., 1 : depth + 1], padded[..., 2 : depth + 2]], 0
    )


def stack_reverse(source):
    depth = source.shape[-1]
    padded = jnp.pad(source, ((0, 0), (0, 0), (0, 0), (1, 1)))
    return jnp.concatenate(
        [padded[..., 2 : depth + 2], padded[..., 1 : depth + 1], padded[..., 0:depth]], 0
    )


def conv_pad(source, kernel, size_x, size_y):
    stacked = stack_depth(source)
    folded = kernel.reshape(3, 3, 3 * kernel.shape[3], kernel.shape[4])
    total = None
    for row_off in range(3):
        for col_off in range(3):
            window = stacked[:, row_off : row_off + size_x, col_off : col_off + size_y]
            term = jnp.einsum(
                "co,cxyz->oxyz",
                folded[row_off, col_off],
                window,
                preferred_element_type=jnp.float32,
            )
            total = term if total is None else total + term
    return total


def grad_forward(source, grad, size_x, size_y):
    stacked = stack_depth(source)
    pieces = []
    for row_off in range(3):
        for col_off in range(3):
            window = stacked[:, row_off : row_off + size_x, col_off : col_off + size_y]
            pieces.append(
                jnp.einsum("cxyz,oxyz->co", window, grad, preferred_element_type=jnp.float32)
            )
    return jnp.stack(pieces, 0).reshape(3, 3, 3, source.shape[0], grad.shape[0])


def grad_backward(activ, grad_pad, size_x, size_y):
    stacked = stack_reverse(grad_pad)
    pieces = []
    for row_off in range(3):
        for col_off in range(3):
            start_x = 2 - row_off
            start_y = 2 - col_off
            window = stacked[:, start_x : start_x + size_x, start_y : start_y + size_y]
            block = jnp.einsum("cxyz,kxyz->ck", activ, window, preferred_element_type=jnp.float32)
            block = block.reshape(activ.shape[0], 3, grad_pad.shape[0])
            pieces.append(jnp.transpose(block, (1, 0, 2)))
    return jnp.stack(pieces, 0).reshape(3, 3, 3, activ.shape[0], grad_pad.shape[0])


def shards(features, cotangent, block_mask, kernel_one, kernel_two):
    chans, tile_x, tile_y, tile_z = features.shape
    cell = upsample(block_mask).astype(jnp.bfloat16)[None]
    cell_f = cell.astype(jnp.float32)
    masked_in = features * cell
    masked_grad = cotangent * cell
    flip_one = flip_kernel(kernel_one)
    flip_two = flip_kernel(kernel_two)
    cells_all = tile_x * tile_y * tile_z * lax.axis_size("gx") * lax.axis_size("gy")
    scale = 1.0 / math.sqrt(cells_all)
    in_pad, grad_pad = (
        padded_2(masked_in, (("gx", 1), ("gy", 2)), 1),
        padded_2(masked_grad, (("gx", 1), ("gy", 2)), 1),
    )
    pre_act = conv_pad(in_pad, kernel_one, tile_x, tile_y)
    activ = (cell_f * jax.nn.silu(pre_act)).astype(jnp.bfloat16)
    partial_two = grad_backward(activ, grad_pad, tile_x, tile_y)
    summed_two = partial_two
    act_grad = conv_pad(grad_pad, flip_two, tile_x, tile_y)
    pre_grad = (cell_f * silu_slope(pre_act) * act_grad).astype(jnp.bfloat16)
    hidden_pad = padded_2(pre_grad, (("gx", 1), ("gy", 2)), 1)
    partial_one = grad_forward(in_pad, pre_grad, tile_x, tile_y)
    branch = conv_pad(hidden_pad, flip_one, tile_x, tile_y)
    grad_features = (cell_f * (cotangent.astype(jnp.float32) + branch)).astype(jnp.bfloat16)
    summed_one, summed_two = lax.psum((partial_one, summed_two), ("gx", "gy"))
    return (grad_features, summed_one * scale, summed_two * scale)


def solution(mesh):
    placed = (P(None, "gx", "gy", None), P(None, "gx", "gy", None), P("gx", "gy", None), P(), P())
    return jax.shard_map(
        shards,
        mesh=mesh,
        in_specs=placed,
        out_specs=(P(None, "gx", "gy", None), P(), P()),
        check_vma=False,
    )
```

profile of v0, /device:TPU:1, one launch (start us, length us, event | category | flops | bytes accessed | tf_op | source)
XLA Modules:
  0.0 286.3 jit_solution(6869526273240850333)
XLA Ops:
  8.1 3.3 %copy_multiply_fusion.1 = (bf16[64,8,8,128]{3,0,2,1:T(8,128)(2,1)S(1)}, bf16[64,8,8,128]{3,0,2,1:T(8,128)(2,1)S(1)}) fusion(bf16[64,8,8,128]{3,2,1,0:T(8,128)(2,1)} %param.6, bf16[128]{0:T(256)(128)(2,1)S(1)} %convert_element_type.40, bf16[64,8,8,128]{3,2,1,0:T(8,128)(2,1)} %param.5), kind=kLoop, calls=%fused_computation.141 | loop fusion | flops 1048576 | bytes 4194560 | tf_op jit(solution)/shard_map/mul | solution.py:106
  11.5 4.5 %collective-permute-start = (bf16[64,1,8,128]{3,0,2,1:T(8,128)(2,1)S(1)}, bf16[64,1,8,128]{3,0,2,1:T(8,128)(2,1)S(1)}, u32[]{:S(2)}, u32[]{:S(2)}) collective-permute-start(bf16[64,1,8,128]{3,0,2,1:T(8,128)(2,1)S(1)} %get-tuple-element.29), channel_id=1, source_target_pairs={{0,8},{8,16},{16,24},{24,32},{32,40},{40,48},{48,56},{56,64},{64,7... | collective-permute-start | bytes 393224 | tf_op jit(solution)/shard_map/ppermute | solution.py:18
  16.0 1.9 collective-permute-start.1
  18.6 3.8 %collective-permute-start.4 = (bf16[64,1,8,128]{3,0,2,1:T(8,128)(2,1)}, bf16[64,1,8,128]{3,0,2,1:T(8,128)(2,1)S(1)}, u32[]{:S(2)}, u32[]{:S(2)}) collective-permute-start(bf16[64,1,8,128]{3,0,2,1:T(8,128)(2,1)} %get-tuple-element.27), channel_id=1, source_target_pairs={{0,8},{8,16},{16,24},{24,32},{32,40},{40,48},{48,56},{56,64},{64,7... | collective-permute-start | bytes 393224 | tf_op jit(solution)/shard_map/ppermute | solution.py:18
  22.4 1.9 collective-permute-start.5
  24.4 0.8 pad_maximum_fusion.13
  25.2 6.2 %collective-permute-start.2 = (bf16[64,10,1,128]{3,0,2,1:T(8,128)(2,1)}, bf16[64,10,1,128]{3,0,2,1:T(8,128)(2,1)}, u32[]{:S(2)}, u32[]{:S(2)}) collective-permute-start(bf16[64,10,1,128]{3,0,2,1:T(8,128)(2,1)} %get-tuple-element.23), channel_id=1, source_target_pairs={{0,1},{1,2},{2,3},{3,4},{4,5},{5,6},{6,7},{8,9},{9,10},{10,11},{11... | collective-permute-start | bytes 491528 | tf_op jit(solution)/shard_map/ppermute | solution.py:18
  31.4 1.3 collective-permute-start.3
  33.2 1.0 copy.29
  34.2 1.0 copy.39
  35.1 0.8 pad_maximum_fusion.10
  35.9 5.5 %collective-permute-start.6 = (bf16[64,10,1,128]{3,0,2,1:T(8,128)(2,1)S(1)}, bf16[64,10,1,128]{3,0,2,1:T(8,128)(2,1)S(1)}, u32[]{:S(2)}, u32[]{:S(2)}) collective-permute-start(bf16[64,10,1,128]{3,0,2,1:T(8,128)(2,1)S(1)} %get-tuple-element.21), channel_id=1, source_target_pairs={{0,1},{1,2},{2,3},{3,4},{4,5},{5,6},{6,7},{8,9},{9,10},{10,11},{11... | collective-permute-start | bytes 491528 | tf_op jit(solution)/shard_map/ppermute | solution.py:18
  41.4 1.8 collective-permute-start.7
  43.2 4.0 %fusion.15 = bf16[64,10,10,130]{3,0,2,1:T(8,128)(2,1)S(1)} fusion(bf16[64,10,1,128]{3,0,2,1:T(8,128)(2,1)} %collective-permute-done.3, bf16[64,10,1,128]{3,0,2,1:T(8,128)(2,1)} %collective-permute-done.2, bf16[64,1,8,128]{3,0,2,1:T(8,128)(2,1)} %copy-done.6, bf16[64,8,8,128]{3,0,2,1:T(8,128)(2,1)S(1)} %get-tuple-element.32, bf16[64,1,8,128]{3,0,2,1:T(8,128)(2,1)} %copy-done.4), kind=kLoop, calls=%fused_computation.24 | loop fusion | flops 14976000 | bytes 3302400 | tf_op jit(solution)/shard_map/concatenate | solution.py:16
  47.3 0.9 fusion.124
  48.2 4.9 %pad_maximum_fusion = bf16[192,10,10,128]{3,0,2,1:T(8,128)(2,1)S(1)} fusion(bf16[64,10,10,128]{3,0,2,1:T(8,128)(2,1)S(1)} %get-tuple-element.18, bf16[64,10,1,128]{3,0,2,1:T(8,128)(2,1)} %collective-permute-done.3, bf16[64,1,8,128]{3,0,2,1:T(8,128)(2,1)S(1)} %copy-done.7, bf16[64,8,8,128]{3,0,2,1:T(8,128)(2,1)S(1)} %get-tuple-element.32, ...), kind=kLoop, calls=%fused_computation.3 | loop fusion | flops 34406400 | bytes 9830400 | tf_op jit(solution)/shard_map/concatenate | solution.py:45
  54.6 0.7 fusion.84
  55.3 0.7 fusion.86
  56.1 0.7 fusion.88
  57.6 0.7 fusion.92
  59.1 3.9 %fusion.19 = bf16[64,10,10,130]{3,0,2,1:T(8,128)(2,1)S(1)} fusion(bf16[64,10,1,128]{3,0,2,1:T(8,128)(2,1)S(1)} %collective-permute-done.7, bf16[64,10,1,128]{3,0,2,1:T(8,128)(2,1)S(1)} %collective-permute-done.6, bf16[64,1,8,128]{3,0,2,1:T(8,128)(2,1)} %collective-permute-done.5, bf16[64,8,8,128]{3,0,2,1:T(8,128)(2,1)S(1)} %get-tuple-element.31, ...), kind=kLoop, calls=%fused_computation.28 | loop fusion | flops 14976000 | bytes 3302400 | tf_op jit(solution)/shard_map/concatenate | solution.py:16
  63.0 2.1 fusion.123
  65.1 1.7 fusion.106
  66.9 5.4 %pad_maximum_fusion.4 = (bf16[192,10,10,128]{3,0,2,1:T(8,128)(2,1)S(1)}, bf16[192,10,10,128]{3,0,2,1:T(8,128)(2,1)S(1)}) fusion(bf16[64,10,10,128]{3,0,2,1:T(8,128)(2,1)S(1)} %get-tuple-element.15, bf16[64,10,10,128]{3,0,2,1:T(8,128)(2,1)} %get-tuple-element.16, bf16[64,10,1,128]{3,0,2,1:T(8,128)(2,1)S(1)} %collective-permute-done.7, ...), kind=kLoop, calls=%fused_computation.7 | loop fusion | flops 46694400 | bytes 14745600 | tf_op jit(solution)/shard_map/concatenate | solution.py:53
  72.3 1.0 fusion.24
  73.3 1.0 fusion.26
  74.2 1.0 fusion.28
  75.2 1.0 fusion.30
  76.1 1.0 fusion.32
  77.1 1.0 fusion.34
  78.1 1.0 fusion.36
  79.0 1.0 fusion.38
  80.0 1.6 fusion.40
  82.4 0.7 fusion.64
  83.1 0.7 fusion.66
  83.8 0.7 fusion.68
  84.6 0.7 fusion.70
  85.3 0.7 fusion.72
  86.1 0.7 fusion.74
  86.8 2.1 fusion.76
  88.9 3.5 %fusion.98 = bf16[64,8,8,128]{3,0,2,1:T(8,128)(2,1)S(1)} fusion(f32[8,8,128,64]{2,3,1,0:T(8,128)S(1)} %get-tuple-element.34, f32[8,8,128,64]{2,3,1,0:T(8,128)S(1)} %fusion.62, f32[8,8,128,64]{2,3,1,0:T(8,128)S(1)} %fusion.64, f32[8,8,128,64]{2,3,1,0:T(8,128)S(1)} %fusion.66, f32[8,8,128,64]{2,3,1,0:T(8,128)S(1)} %fusion.68, ...), kind=kOutput, calls=%fused_computation.109 | convolution fusion | flops 210763776 | bytes 23118336 | tf_op jit(solution)/shard_map/co,cxyz->oxyz/dot_general | solution.py:65
  92.5 1.1 fusion.115
  93.6 4.5 %collective-permute-start.8 = (bf16[64,1,8,128]{3,0,2,1:T(8,128)(2,1)S(1)}, bf16[64,1,8,128]{3,0,2,1:T(8,128)(2,1)S(1)}, u32[]{:S(2)}, u32[]{:S(2)}) collective-permute-start(bf16[64,1,8,128]{3,0,2,1:T(8,128)(2,1)S(1)} %get-tuple-element.25), channel_id=1, source_target_pairs={{0,8},{8,16},{16,24},{24,32},{32,40},{40,48},{48,56},{56,64},{64,7... | collective-permute-start | bytes 393224 | tf_op jit(solution)/shard_map/ppermute | solution.py:18
  98.1 1.9 collective-permute-start.9
  100.1 1.1 fusion.114
  101.2 1.1 fusion.113
  102.3 1.1 fusion.112
  103.4 1.1 fusion.111
  104.5 1.1 fusion.110
  105.6 1.1 fusion.109
  106.7 1.1 fusion.108
  107.8 1.1 fusion.107
  109.1 5.8 %collective-permute-start.10 = (bf16[64,10,1,128]{3,0,2,1:T(8,128)(2,1)S(1)}, bf16[64,10,1,128]{3,0,2,1:T(8,128)(2,1)S(1)}, u32[]{:S(2)}, u32[]{:S(2)}) collective-permute-start(bf16[64,10,1,128]{3,0,2,1:T(8,128)(2,1)S(1)} %get-tuple-element.19), channel_id=1, source_target_pairs={{0,1},{1,2},{2,3},{3,4},{4,5},{5,6},{6,7},{8,9},{9,10},{10,11},{11... | collective-permute-start | bytes 491528 | tf_op jit(solution)/shard_map/ppermute | solution.py:18
  114.9 1.5 collective-permute-start.11
  116.5 1.2 copy.59
  117.7 1.2 copy.49
  118.9 3.6 %collective-permute-done.11 = bf16[64,10,1,128]{3,0,2,1:T(8,128)(2,1)S(1)} collective-permute-done((bf16[64,10,1,128]{3,0,2,1:T(8,128)(2,1)S(1)}, bf16[64,10,1,128]{3,0,2,1:T(8,128)(2,1)S(1)}, u32[]{:S(2)}, u32[]{:S(2)}) %collective-permute-start.11) | collective-permute-done | bytes 163872 | tf_op jit(solution)/shard_map/ppermute | solution.py:20
  122.5 3.1 %select_maximum_fusion = bf16[64,10,10,130]{3,0,2,1:T(8,128)(2,1)S(1)} fusion(bf16[64,10,1,128]{3,0,2,1:T(8,128)(2,1)S(1)} %collective-permute-done.11, bf16[64,10,1,128]{3,0,2,1:T(8,128)(2,1)S(1)} %collective-permute-done.10, bf16[64,1,8,128]{3,0,2,1:T(8,128)(2,1)S(1)} %collective-permute-done.9, bf16[64,8,8,128]{3,0,2,1:T(8,128)(2,1)S(1)} %fusion.98, ...), kind=kLoop, calls=%fused_computation.8 | loop fusion | flops 14976000 | bytes 3302400 | tf_op jit(solution)/shard_map/concatenate | solution.py:16
  125.6 0.9 fusion.122
  126.5 4.3 %pad_maximum_fusion.3 = bf16[192,10,10,128]{3,0,2,1:T(8,128)(2,1)S(1)} fusion(bf16[64,10,10,128]{3,0,2,1:T(8,128)(2,1)S(1)} %get-tuple-element.14, bf16[64,10,1,128]{3,0,2,1:T(8,128)(2,1)S(1)} %collective-permute-done.11, bf16[64,1,8,128]{3,0,2,1:T(8,128)(2,1)S(1)} %collective-permute-done.9, bf16[64,8,8,128]{3,0,2,1:T(8,128)(2,1)S(1)} %fusion.98, ...), kind=kLoop, calls=%fused_computation.6 | loop fusion | flops 34406400 | bytes 9830400 | tf_op jit(solution)/shard_map/concatenate | solution.py:45
  137.2 2.2 fusion.97
  139.5 1.6 copy.60
  141.1 135.2 %all-reduce.6.cloned.1.call-done = (f32[3,3,3,64,64]{4,3,2,1,0:T(8,128)}, f32[3,3,3,64,64]{4,3,2,1,0:T(8,128)}) async-done(((f32[3,3,3,64,64]{4,3,2,1,0:T(8,128)}, f32[3,3,3,64,64]{4,3,2,1,0:T(8,128)}), (f32[3,3,3,64,64]{4,3,2,1,0:T(8,128)}, f32[3,3,3,64,64]{4,3,2,1,0:T(8,128)})) %all-reduce.6.cloned.1.call-update) | async-done | bytes 884752 | tf_op jit(solution)/shard_map/psum | solution.py:125
  276.3 2.9 %broadcast_multiply_fusion = (f32[3,3,3,64,64]{4,3,2,1,0:T(8,128)}, f32[3,3,3,64,64]{4,3,2,1,0:T(8,128)}) fusion(f32[3,3,3,64,64]{4,3,2,1,0:T(8,128)} %get-tuple-element.10, f32[3,3,3,64,64]{4,3,2,1,0:T(8,128)} %get-tuple-element.9), kind=kLoop, calls=%fused_computation.142 | loop fusion | flops 221184 | bytes 1769472 | tf_op jit(solution)/shard_map/mul | solution.py:126
  (71 shorter events, 12.6 us)
Async XLA Ops:
  7.2 17.2 %copy-start.8 = (bf16[3,3,3,64,64]{4,3,2,1,0:T(8,128)(2,1)S(1)}, bf16[3,3,3,64,64]{4,3,2,1,0:T(8,128)(2,1)}, u32[]{:S(2)}) copy-start(bf16[3,3,3,64,64]{4,3,2,1,0:T(8,128)(2,1)} %param.9) | copy-start | bytes 663556
  7.2 269.2 %all-reduce.6.cloned.1.call-start = ((), (), s32[]{:S(2)}) async-start(), calls=%async_computation | async-start | bytes 3538944 | tf_op jit(solution)/shard_map/psum | solution.py:125
  8.1 10.5 %copy-start.11 = (bf16[128]{0:T(256)(128)(2,1)}, bf16[128]{0:T(256)(128)(2,1)S(1)}, u32[]{:S(2)}) copy-start(bf16[128]{0:T(256)(128)(2,1)S(1)} %convert_element_type.40) | copy-start | bytes 772
  8.1 24.5 %copy-start.1 = (bf16[3,3,3,64,64]{4,3,2,1,0:T(8,128)(2,1)S(1)}, bf16[3,3,3,64,64]{4,3,2,1,0:T(8,128)(2,1)}, u32[]{:S(2)}) copy-start(bf16[3,3,3,64,64]{4,3,2,1,0:T(8,128)(2,1)} %param.8) | copy-start | bytes 663556
  11.5 12.9 %collective-permute-start = (bf16[64,1,8,128]{3,0,2,1:T(8,128)(2,1)S(1)}, bf16[64,1,8,128]{3,0,2,1:T(8,128)(2,1)S(1)}, u32[]{:S(2)}, u32[]{:S(2)}) collective-permute-start(bf16[64,1,8,128]{3,0,2,1:T(8,128)(2,1)S(1)} %get-tuple-element.29), channel_id=1, source_target_pairs={{0,8},{8,16},{16,24},{24,32},{32,40},{40,48},{48,56},{56,64},{64,7... | collective-permute-start | bytes 393224 | tf_op jit(solution)/shard_map/ppermute | solution.py:18
  16.0 8.4 %collective-permute-start.1 = (bf16[64,1,8,128]{3,0,2,1:T(8,128)(2,1)S(1)}, bf16[64,1,8,128]{3,0,2,1:T(8,128)(2,1)S(1)}, u32[]{:S(2)}, u32[]{:S(2)}) collective-permute-start(bf16[64,1,8,128]{3,0,2,1:T(8,128)(2,1)S(1)} %get-tuple-element.30), channel_id=1, source_target_pairs={{8,0},{16,8},{24,16},{32,24},{40,32},{48,40},{56,48},{64,56},{72,6... | collective-permute-start | bytes 393224 | tf_op jit(solution)/shard_map/ppermute | solution.py:20
  18.6 14.1 %copy-start.12 = (bf16[128]{0:T(256)(128)(2,1)S(1)}, bf16[128]{0:T(256)(128)(2,1)}, u32[]{:S(2)}) copy-start(bf16[128]{0:T(256)(128)(2,1)} %copy-done.11) | copy-start | bytes 772
  18.6 16.5 %collective-permute-start.4 = (bf16[64,1,8,128]{3,0,2,1:T(8,128)(2,1)}, bf16[64,1,8,128]{3,0,2,1:T(8,128)(2,1)S(1)}, u32[]{:S(2)}, u32[]{:S(2)}) collective-permute-start(bf16[64,1,8,128]{3,0,2,1:T(8,128)(2,1)} %get-tuple-element.27), channel_id=1, source_target_pairs={{0,8},{8,16},{16,24},{24,32},{32,40},{40,48},{48,56},{56,64},{64,7... | collective-permute-start | bytes 393224 | tf_op jit(solution)/shard_map/ppermute | solution.py:18
  22.4 12.7 %collective-permute-start.5 = (bf16[64,1,8,128]{3,0,2,1:T(8,128)(2,1)}, bf16[64,1,8,128]{3,0,2,1:T(8,128)(2,1)}, u32[]{:S(2)}, u32[]{:S(2)}) collective-permute-start(bf16[64,1,8,128]{3,0,2,1:T(8,128)(2,1)} %get-tuple-element.28), channel_id=1, source_target_pairs={{8,0},{16,8},{24,16},{32,24},{40,32},{48,40},{56,48},{64,56},{72,6... | collective-permute-start | bytes 393224 | tf_op jit(solution)/shard_map/ppermute | solution.py:20
  24.4 7.0 %copy-start.4 = (bf16[64,1,8,128]{3,0,2,1:T(8,128)(2,1)}, bf16[64,1,8,128]{3,0,2,1:T(8,128)(2,1)S(1)}, u32[]{:S(2)}) copy-start(bf16[64,1,8,128]{3,0,2,1:T(8,128)(2,1)S(1)} %collective-permute-done) | copy-start | bytes 393220
  24.4 8.2 %copy-start.6 = (bf16[64,1,8,128]{3,0,2,1:T(8,128)(2,1)}, bf16[64,1,8,128]{3,0,2,1:T(8,128)(2,1)S(1)}, u32[]{:S(2)}) copy-start(bf16[64,1,8,128]{3,0,2,1:T(8,128)(2,1)S(1)} %collective-permute-done.1) | copy-start | bytes 393220
  25.2 18.0 %collective-permute-start.2 = (bf16[64,10,1,128]{3,0,2,1:T(8,128)(2,1)}, bf16[64,10,1,128]{3,0,2,1:T(8,128)(2,1)}, u32[]{:S(2)}, u32[]{:S(2)}) collective-permute-start(bf16[64,10,1,128]{3,0,2,1:T(8,128)(2,1)} %get-tuple-element.23), channel_id=1, source_target_pairs={{0,1},{1,2},{2,3},{3,4},{4,5},{5,6},{6,7},{8,9},{9,10},{10,11},{11... | collective-permute-start | bytes 491528 | tf_op jit(solution)/shard_map/ppermute | solution.py:18
  31.4 11.9 %collective-permute-start.3 = (bf16[64,10,1,128]{3,0,2,1:T(8,128)(2,1)}, bf16[64,10,1,128]{3,0,2,1:T(8,128)(2,1)}, u32[]{:S(2)}, u32[]{:S(2)}) collective-permute-start(bf16[64,10,1,128]{3,0,2,1:T(8,128)(2,1)} %get-tuple-element.24), channel_id=1, source_target_pairs={{1,0},{2,1},{3,2},{4,3},{5,4},{6,5},{7,6},{9,8},{10,9},{11,10},{12... | collective-permute-start | bytes 491528 | tf_op jit(solution)/shard_map/ppermute | solution.py:20
  35.9 23.1 %collective-permute-start.6 = (bf16[64,10,1,128]{3,0,2,1:T(8,128)(2,1)S(1)}, bf16[64,10,1,128]{3,0,2,1:T(8,128)(2,1)S(1)}, u32[]{:S(2)}, u32[]{:S(2)}) collective-permute-start(bf16[64,10,1,128]{3,0,2,1:T(8,128)(2,1)S(1)} %get-tuple-element.21), channel_id=1, source_target_pairs={{0,1},{1,2},{2,3},{3,4},{4,5},{5,6},{6,7},{8,9},{9,10},{10,11},{11... | collective-permute-start | bytes 491528 | tf_op jit(solution)/shard_map/ppermute | solution.py:18
  41.4 17.6 %collective-permute-start.7 = (bf16[64,10,1,128]{3,0,2,1:T(8,128)(2,1)S(1)}, bf16[64,10,1,128]{3,0,2,1:T(8,128)(2,1)S(1)}, u32[]{:S(2)}, u32[]{:S(2)}) collective-permute-start(bf16[64,10,1,128]{3,0,2,1:T(8,128)(2,1)S(1)} %get-tuple-element.22), channel_id=1, source_target_pairs={{1,0},{2,1},{3,2},{4,3},{5,4},{6,5},{7,6},{9,8},{10,9},{11,10},{12... | collective-permute-start | bytes 491528 | tf_op jit(solution)/shard_map/ppermute | solution.py:20
  47.2 0.9 copy-start.5
  47.2 1.0 copy-start.7
  63.0 2.1 copy-start.10
  80.0 1.6 copy-start.3
  92.5 1.2 copy-start.9
  93.6 15.4 %collective-permute-start.8 = (bf16[64,1,8,128]{3,0,2,1:T(8,128)(2,1)S(1)}, bf16[64,1,8,128]{3,0,2,1:T(8,128)(2,1)S(1)}, u32[]{:S(2)}, u32[]{:S(2)}) collective-permute-start(bf16[64,1,8,128]{3,0,2,1:T(8,128)(2,1)S(1)} %get-tuple-element.25), channel_id=1, source_target_pairs={{0,8},{8,16},{16,24},{24,32},{32,40},{40,48},{48,56},{56,64},{64,7... | collective-permute-start | bytes 393224 | tf_op jit(solution)/shard_map/ppermute | solution.py:18
  98.1 10.9 %collective-permute-start.9 = (bf16[64,1,8,128]{3,0,2,1:T(8,128)(2,1)S(1)}, bf16[64,1,8,128]{3,0,2,1:T(8,128)(2,1)S(1)}, u32[]{:S(2)}, u32[]{:S(2)}) collective-permute-start(bf16[64,1,8,128]{3,0,2,1:T(8,128)(2,1)S(1)} %get-tuple-element.26), channel_id=1, source_target_pairs={{8,0},{16,8},{24,16},{32,24},{40,32},{48,40},{56,48},{64,56},{72,6... | collective-permute-start | bytes 393224 | tf_op jit(solution)/shard_map/ppermute | solution.py:20
  109.1 9.8 %collective-permute-start.10 = (bf16[64,10,1,128]{3,0,2,1:T(8,128)(2,1)S(1)}, bf16[64,10,1,128]{3,0,2,1:T(8,128)(2,1)S(1)}, u32[]{:S(2)}, u32[]{:S(2)}) collective-permute-start(bf16[64,10,1,128]{3,0,2,1:T(8,128)(2,1)S(1)} %get-tuple-element.19), channel_id=1, source_target_pairs={{0,1},{1,2},{2,3},{3,4},{4,5},{5,6},{6,7},{8,9},{9,10},{10,11},{11... | collective-permute-start | bytes 491528 | tf_op jit(solution)/shard_map/ppermute | solution.py:18
  114.9 7.6 %collective-permute-start.11 = (bf16[64,10,1,128]{3,0,2,1:T(8,128)(2,1)S(1)}, bf16[64,10,1,128]{3,0,2,1:T(8,128)(2,1)S(1)}, u32[]{:S(2)}, u32[]{:S(2)}) collective-permute-start(bf16[64,10,1,128]{3,0,2,1:T(8,128)(2,1)S(1)} %get-tuple-element.20), channel_id=1, source_target_pairs={{1,0},{2,1},{3,2},{4,3},{5,4},{6,5},{7,6},{9,8},{10,9},{11,10},{12... | collective-permute-start | bytes 491528 | tf_op jit(solution)/shard_map/ppermute | solution.py:20
  126.5 4.4 %copy-start.2 = (bf16[3,3,3,64,64]{4,3,2,1,0:T(8,128)(2,1)S(1)}, bf16[3,3,3,64,64]{4,3,2,1,0:T(8,128)(2,1)}, u32[]{:S(2)}) copy-start(bf16[3,3,3,64,64]{4,3,2,1,0:T(8,128)(2,1)} %copy.39) | copy-start | bytes 663556
  136.0 1.2 copy-start
Sparse Core Ops, SparseCore 0:
  119.0 157.2 all-reduce.5
where the time goes:
time: 290 us; the launch traced here: 286 us
  waiting for transfers between devices  139 us (48%)
  matrix products  45.8 us (16%)
  starting transfers between devices  40.5 us (14%)
  other arithmetic  34.6 us (12%)
  between operations  14.9 us (5%)
  local copies, waits for them, and re-layouts  11.6 us (4%)
    psum x1, waiting for transfers between devices, shards(): summed_one, summed_two = lax.psum((partial_one, summed_two), ('gx', 'gy'))  135 us
    ppermute x6, starting transfers between devices, padded_2(): lax.ppermute(tail, axis, [(i, (i + 1) % count) for i in range(ends)])  30.2 us
    dot_general x27, matrix products, conv_pad(): jnp.einsum('co,cxyz->oxyz', folded[row_off, col_off], window, preferred_e...  26.6 us
    concatenate x3, other arithmetic, padded_2(): jnp.concatenate([lax.ppermute(tail, axis, [(i, (i + 1) % count) for i in...  11 us
    ppermute x6, starting transfers between devices, padded_2(): lax.ppermute(head, axis, [((i + 1) % count, i) for i in range(ends)])  10.3 us
    dot_general x9, matrix products, grad_forward(): jnp.einsum('cxyz,oxyz->co', window, grad, preferred_element_type=jnp.floa...  10 us
    dot_general x9, matrix products, grad_backward(): jnp.einsum('cxyz,kxyz->ck', activ, window, preferred_element_type=jnp.flo...  9.26 us
    concatenate x2, other arithmetic, stack_depth(): jnp.concatenate([padded[..., 0:depth], padded[..., 1:depth + 1], padded[....  9.24 us
  transfers between devices with their start and end apart: 13, of which 2 were waited for; matrix products, arithmetic and copies ran while one was open for 17% of the time, Pallas kernels for 0%

commit v1 on v0

--- a/solution.py
+++ b/solution.py
@@ -122,7 +122,7 @@
     partial_one = grad_forward(in_pad, pre_grad, tile_x, tile_y)
     branch = conv_pad(hidden_pad, flip_one, tile_x, tile_y)
     grad_features = (cell_f * (cotangent.astype(jnp.float32) + branch)).astype(jnp.bfloat16)
-    summed_one, summed_two = lax.psum((partial_one, summed_two), ("gx", "gy"))
+    summed_one, summed_two = lax.psum(lax.psum((partial_one, summed_two), "gy"), "gx")
     return (grad_features, summed_one * scale, summed_two * scale)
 
 

time: 290 us -> 366 us (1.26)
  waiting for transfers between devices: 139 us -> 200 us
  matrix products: 45.8 us -> 61.4 us
    psum x1 -> x2, waiting for transfers between devices: 135 us -> 196 us  [the longest x1 118 us: shards(): lax.psum(lax.psum((partial_one, summed_two), 'gy'), 'gx')]
    dot_general x27, matrix products: 26.6 us -> 42.1 us  [conv_pad(): jnp.einsum('co,cxyz->oxyz', folded[row_off, col_off], window, preferred_e...]
  transfers between devices with their start and end apart: 13 -> 14, of which waited for: 2 -> 3; matrix products, arithmetic and copies ran while one was open for 17% -> 18% of each run, Pallas kernels for 0% -> 0%
where the time goes in v1:
time: 366 us; the launch traced here: 362 us
  waiting for transfers between devices  200 us (55%)
  matrix products  61.4 us (17%)
  starting transfers between devices  40.4 us (11%)
  other arithmetic  34.7 us (9%)
  between operations  14.9 us (4%)
  local copies, waits for them, and re-layouts  11.1 us (3%)
    psum x1, waiting for transfers between devices, shards(): lax.psum(lax.psum((partial_one, summed_two), 'gy'), 'gx')  118 us
    psum x1, waiting for transfers between devices, shards(): lax.psum((partial_one, summed_two), 'gy')  78.6 us
    dot_general x27, matrix products, conv_pad(): jnp.einsum('co,cxyz->oxyz', folded[row_off, col_off], window, preferred_e...  42.1 us
    ppermute x6, starting transfers between devices, padded_2(): lax.ppermute(tail, axis, [(i, (i + 1) % count) for i in range(ends)])  30 us
    concatenate x3, other arithmetic, padded_2(): jnp.concatenate([lax.ppermute(tail, axis, [(i, (i + 1) % count) for i in...  11 us
    ppermute x6, starting transfers between devices, padded_2(): lax.ppermute(head, axis, [((i + 1) % count, i) for i in range(ends)])  10.1 us
    dot_general x9, matrix products, grad_forward(): jnp.einsum('cxyz,oxyz->co', window, grad, preferred_element_type=jnp.floa...  9.99 us
    concatenate x2, other arithmetic, stack_depth(): jnp.concatenate([padded[..., 0:depth], padded[..., 1:depth + 1], padded[....  9.26 us
  transfers between devices with their start and end apart: 14, of which 3 were waited for; matrix products, arithmetic and copies ran while one was open for 18% of the time, Pallas kernels for 0%

profile of v1, /device:TPU:1, one launch (start us, length us, event | category | flops | bytes accessed | tf_op | source)
XLA Modules:
  0.0 362.2 jit_solution(17886839819134775851)
XLA Ops:
  8.1 3.3 copy_multiply_fusion.1
  11.5 4.5 %collective-permute-start = (bf16[64,1,8,128]{3,0,2,1:T(8,128)(2,1)S(1)}, bf16[64,1,8,128]{3,0,2,1:T(8,128)(2,1)S(1)}, u32[]{:S(2)}, u32[]{:S(2)}) collective-permute-start(bf16[64,1,8,128]{3,0,2,1:T(8,128)(2,1)S(1)} %get-tuple-element.31), channel_id=1, source_target_pairs={{0,8},{8,16},{16,24},{24,32},{32,40},{40,48},{48,56},{56,64},{64,7... | collective-permute-start | bytes 393224 | tf_op jit(solution)/shard_map/ppermute | solution.py:18
  16.0 1.9 collective-permute-start.1
  18.6 3.6 %collective-permute-start.4 = (bf16[64,1,8,128]{3,0,2,1:T(8,128)(2,1)}, bf16[64,1,8,128]{3,0,2,1:T(8,128)(2,1)S(1)}, u32[]{:S(2)}, u32[]{:S(2)}) collective-permute-start(bf16[64,1,8,128]{3,0,2,1:T(8,128)(2,1)} %get-tuple-element.29), channel_id=1, source_target_pairs={{0,8},{8,16},{16,24},{24,32},{32,40},{40,48},{48,56},{56,64},{64,7... | collective-permute-start | bytes 393224 | tf_op jit(solution)/shard_map/ppermute | solution.py:18
  22.3 1.9 collective-permute-start.5
  24.3 0.8 pad_maximum_fusion.13
  25.1 6.2 %collective-permute-start.2 = (bf16[64,10,1,128]{3,0,2,1:T(8,128)(2,1)}, bf16[64,10,1,128]{3,0,2,1:T(8,128)(2,1)}, u32[]{:S(2)}, u32[]{:S(2)}) collective-permute-start(bf16[64,10,1,128]{3,0,2,1:T(8,128)(2,1)} %get-tuple-element.25), channel_id=1, source_target_pairs={{0,1},{1,2},{2,3},{3,4},{4,5},{5,6},{6,7},{8,9},{9,10},{10,11},{11... | collective-permute-start | bytes 491528 | tf_op jit(solution)/shard_map/ppermute | solution.py:18
  31.2 1.3 collective-permute-start.3
  33.1 1.0 copy.29
  34.1 1.0 copy.39
  35.0 0.8 pad_maximum_fusion.10
  35.8 5.5 %collective-permute-start.6 = (bf16[64,10,1,128]{3,0,2,1:T(8,128)(2,1)S(1)}, bf16[64,10,1,128]{3,0,2,1:T(8,128)(2,1)S(1)}, u32[]{:S(2)}, u32[]{:S(2)}) collective-permute-start(bf16[64,10,1,128]{3,0,2,1:T(8,128)(2,1)S(1)} %get-tuple-element.23), channel_id=1, source_target_pairs={{0,1},{1,2},{2,3},{3,4},{4,5},{5,6},{6,7},{8,9},{9,10},{10,11},{11... | collective-permute-start | bytes 491528 | tf_op jit(solution)/shard_map/ppermute | solution.py:18
  41.3 1.8 collective-permute-start.7
  43.1 4.0 %fusion.15 = bf16[64,10,10,130]{3,0,2,1:T(8,128)(2,1)S(1)} fusion(bf16[64,10,1,128]{3,0,2,1:T(8,128)(2,1)} %collective-permute-done.3, bf16[64,10,1,128]{3,0,2,1:T(8,128)(2,1)} %collective-permute-done.2, bf16[64,1,8,128]{3,0,2,1:T(8,128)(2,1)} %copy-done.7, bf16[64,8,8,128]{3,0,2,1:T(8,128)(2,1)S(1)} %get-tuple-element.34, bf16[64,1,8,128]{3,0,2,1:T(8,128)(2,1)} %copy-done.5), kind=kLoop, calls=%fused_computation.24 | loop fusion | flops 14976000 | bytes 3302400 | tf_op jit(solution)/shard_map/concatenate | solution.py:16
  47.2 0.9 fusion.124
  48.1 4.9 %pad_maximum_fusion = bf16[192,10,10,128]{3,0,2,1:T(8,128)(2,1)S(1)} fusion(bf16[64,10,10,128]{3,0,2,1:T(8,128)(2,1)S(1)} %get-tuple-element.20, bf16[64,10,1,128]{3,0,2,1:T(8,128)(2,1)} %collective-permute-done.3, bf16[64,1,8,128]{3,0,2,1:T(8,128)(2,1)S(1)} %copy-done.8, bf16[64,8,8,128]{3,0,2,1:T(8,128)(2,1)S(1)} %get-tuple-element.34, ...), kind=kLoop, calls=%fused_computation.3 | loop fusion | flops 34406400 | bytes 9830400 | tf_op jit(solution)/shard_map/concatenate | solution.py:45
  55.2 0.7 fusion.86
  56.7 0.7 fusion.90
  59.0 3.9 %fusion.19 = bf16[64,10,10,130]{3,0,2,1:T(8,128)(2,1)S(1)} fusion(bf16[64,10,1,128]{3,0,2,1:T(8,128)(2,1)S(1)} %collective-permute-done.7, bf16[64,10,1,128]{3,0,2,1:T(8,128)(2,1)S(1)} %collective-permute-done.6, bf16[64,1,8,128]{3,0,2,1:T(8,128)(2,1)} %collective-permute-done.5, bf16[64,8,8,128]{3,0,2,1:T(8,128)(2,1)S(1)} %get-tuple-element.33, ...), kind=kLoop, calls=%fused_computation.28 | loop fusion | flops 14976000 | bytes 3302400 | tf_op jit(solution)/shard_map/concatenate | solution.py:16
  62.9 2.1 fusion.123
  65.0 1.7 fusion.106
  66.8 5.5 %pad_maximum_fusion.4 = (bf16[192,10,10,128]{3,0,2,1:T(8,128)(2,1)S(1)}, bf16[192,10,10,128]{3,0,2,1:T(8,128)(2,1)S(1)}) fusion(bf16[64,10,10,128]{3,0,2,1:T(8,128)(2,1)S(1)} %get-tuple-element.17, bf16[64,10,10,128]{3,0,2,1:T(8,128)(2,1)} %get-tuple-element.18, bf16[64,10,1,128]{3,0,2,1:T(8,128)(2,1)S(1)} %collective-permute-done.7, ...), kind=kLoop, calls=%fused_computation.7 | loop fusion | flops 46694400 | bytes 14745600 | tf_op jit(solution)/shard_map/concatenate | solution.py:53
  72.2 1.0 fusion.24
  73.2 1.0 fusion.26
  74.2 1.0 fusion.28
  75.1 1.0 fusion.30
  76.1 1.0 fusion.32
  77.1 1.0 fusion.34
  78.0 1.0 fusion.36
  79.0 1.0 fusion.38
  80.0 1.6 fusion.40
  86.8 2.1 fusion.76
  88.9 3.5 fusion.98
  92.4 1.1 fusion.115
  93.6 4.5 %collective-permute-start.8 = (bf16[64,1,8,128]{3,0,2,1:T(8,128)(2,1)S(1)}, bf16[64,1,8,128]{3,0,2,1:T(8,128)(2,1)S(1)}, u32[]{:S(2)}, u32[]{:S(2)}) collective-permute-start(bf16[64,1,8,128]{3,0,2,1:T(8,128)(2,1)S(1)} %get-tuple-element.27), channel_id=1, source_target_pairs={{0,8},{8,16},{16,24},{24,32},{32,40},{40,48},{48,56},{56,64},{64,7... | collective-permute-start | bytes 393224 | tf_op jit(solution)/shard_map/ppermute | solution.py:18
  98.0 1.9 collective-permute-start.9
  100.0 1.1 fusion.114
  101.1 1.1 fusion.113
  102.2 1.1 fusion.112
  103.3 1.1 fusion.111
  104.4 1.1 fusion.110
  105.5 1.1 fusion.109
  106.6 1.1 fusion.108
  107.7 1.1 fusion.107
  109.0 5.8 %collective-permute-start.10 = (bf16[64,10,1,128]{3,0,2,1:T(8,128)(2,1)S(1)}, bf16[64,10,1,128]{3,0,2,1:T(8,128)(2,1)S(1)}, u32[]{:S(2)}, u32[]{:S(2)}) collective-permute-start(bf16[64,10,1,128]{3,0,2,1:T(8,128)(2,1)S(1)} %get-tuple-element.21), channel_id=1, source_target_pairs={{0,1},{1,2},{2,3},{3,4},{4,5},{5,6},{6,7},{8,9},{9,10},{10,11},{11... | collective-permute-start | bytes 491528 | tf_op jit(solution)/shard_map/ppermute | solution.py:18
  114.8 1.3 collective-permute-start.11
  116.2 1.2 copy.59
  117.4 1.2 copy.49
  118.9 3.5 collective-permute-done.11
  122.4 3.1 select_maximum_fusion
  125.5 0.9 fusion.122
  126.4 4.4 %pad_maximum_fusion.3 = bf16[192,10,10,128]{3,0,2,1:T(8,128)(2,1)S(1)} fusion(bf16[64,10,10,128]{3,0,2,1:T(8,128)(2,1)S(1)} %get-tuple-element.16, bf16[64,10,1,128]{3,0,2,1:T(8,128)(2,1)S(1)} %collective-permute-done.11, bf16[64,1,8,128]{3,0,2,1:T(8,128)(2,1)S(1)} %collective-permute-done.9, bf16[64,8,8,128]{3,0,2,1:T(8,128)(2,1)S(1)} %fusion.98, ...), kind=kLoop, calls=%fused_computation.6 | loop fusion | flops 34406400 | bytes 9830400 | tf_op jit(solution)/shard_map/concatenate | solution.py:45
  131.5 2.1 fusion.46
  133.6 2.1 fusion.48
  135.7 2.0 fusion.50
  137.8 2.2 fusion.52
  139.9 2.1 fusion.54
  142.0 2.0 fusion.56
  144.1 2.1 fusion.58
  146.1 78.6 %all-reduce.10.cloned.1.call-done = (f32[3,3,3,64,64]{4,3,2,1,0:T(8,128)}, f32[3,3,3,64,64]{4,3,2,1,0:T(8,128)}) async-done(((f32[3,3,3,64,64]{4,3,2,1,0:T(8,128)}, f32[3,3,3,64,64]{4,3,2,1,0:T(8,128)}), (f32[3,3,3,64,64]{4,3,2,1,0:T(8,128)}, f32[3,3,3,64,64]{4,3,2,1,0:T(8,128)})) %all-reduce.10.cloned.1.call-update) | async-done | bytes 884752 | tf_op jit(solution)/shard_map/psum | solution.py:125
  224.7 8.4 %fusion.97 = bf16[64,8,8,128]{3,0,2,1:T(8,128)(2,1)S(1)} fusion(f32[8,8,128,64]{2,3,1,0:T(8,128)S(1)} %fusion.44, f32[8,8,128,64]{2,3,1,0:T(8,128)} %fusion.46, f32[8,8,128,64]{2,3,1,0:T(8,128)} %fusion.48, f32[8,8,128,64]{2,3,1,0:T(8,128)} %fusion.50, f32[8,8,128,64]{2,3,1,0:T(8,128)} %fusion.52, f32[8,8,128,64]{2,3,1,0:T(8,128)} %fusion.54, ...), kind=kOutput, calls=%fused_computation.107 | convolution fusion | flops 207618048 | bytes 22069760 | tf_op jit(solution)/shard_map/co,cxyz->oxyz/dot_general | solution.py:65
  233.1 1.6 copy.60
  234.8 117.5 %all-reduce.8.cloned.1.call-done = (f32[3,3,3,64,64]{4,3,2,1,0:T(8,128)}, f32[3,3,3,64,64]{4,3,2,1,0:T(8,128)}) async-done(((f32[3,3,3,64,64]{4,3,2,1,0:T(8,128)}, f32[3,3,3,64,64]{4,3,2,1,0:T(8,128)}), (f32[3,3,3,64,64]{4,3,2,1,0:T(8,128)}, f32[3,3,3,64,64]{4,3,2,1,0:T(8,128)})) %all-reduce.8.cloned.1.call-update) | async-done | bytes 884752 | tf_op jit(solution)/shard_map/psum | solution.py:125
  352.3 2.9 broadcast_multiply_fusion
  (78 shorter events, 13.1 us)
Async XLA Ops:
  7.2 217.5 %all-reduce.10.cloned.1.call-start = ((), (), s32[]{:S(2)}) async-start(), calls=%async_computation.1 | async-start | bytes 3538944 | tf_op jit(solution)/shard_map/psum | solution.py:125
  8.0 14.2 %copy-start.13 = (bf16[128]{0:T(256)(128)(2,1)}, bf16[128]{0:T(256)(128)(2,1)S(1)}, u32[]{:S(2)}) copy-start(bf16[128]{0:T(256)(128)(2,1)S(1)} %convert_element_type.40) | copy-start | bytes 772
  8.1 16.1 %copy-start.9 = (bf16[3,3,3,64,64]{4,3,2,1,0:T(8,128)(2,1)S(1)}, bf16[3,3,3,64,64]{4,3,2,1,0:T(8,128)(2,1)}, u32[]{:S(2)}) copy-start(bf16[3,3,3,64,64]{4,3,2,1,0:T(8,128)(2,1)} %param.9) | copy-start | bytes 663556
  8.1 24.5 %copy-start.2 = (bf16[3,3,3,64,64]{4,3,2,1,0:T(8,128)(2,1)S(1)}, bf16[3,3,3,64,64]{4,3,2,1,0:T(8,128)(2,1)}, u32[]{:S(2)}) copy-start(bf16[3,3,3,64,64]{4,3,2,1,0:T(8,128)(2,1)} %param.8) | copy-start | bytes 663556
  11.5 12.8 %collective-permute-start = (bf16[64,1,8,128]{3,0,2,1:T(8,128)(2,1)S(1)}, bf16[64,1,8,128]{3,0,2,1:T(8,128)(2,1)S(1)}, u32[]{:S(2)}, u32[]{:S(2)}) collective-permute-start(bf16[64,1,8,128]{3,0,2,1:T(8,128)(2,1)S(1)} %get-tuple-element.31), channel_id=1, source_target_pairs={{0,8},{8,16},{16,24},{24,32},{32,40},{40,48},{48,56},{56,64},{64,7... | collective-permute-start | bytes 393224 | tf_op jit(solution)/shard_map/ppermute | solution.py:18
  16.0 8.3 %collective-permute-start.1 = (bf16[64,1,8,128]{3,0,2,1:T(8,128)(2,1)S(1)}, bf16[64,1,8,128]{3,0,2,1:T(8,128)(2,1)S(1)}, u32[]{:S(2)}, u32[]{:S(2)}) collective-permute-start(bf16[64,1,8,128]{3,0,2,1:T(8,128)(2,1)S(1)} %get-tuple-element.32), channel_id=1, source_target_pairs={{8,0},{16,8},{24,16},{32,24},{40,32},{48,40},{56,48},{64,56},{72,6... | collective-permute-start | bytes 393224 | tf_op jit(solution)/shard_map/ppermute | solution.py:20
  18.6 16.4 %collective-permute-start.4 = (bf16[64,1,8,128]{3,0,2,1:T(8,128)(2,1)}, bf16[64,1,8,128]{3,0,2,1:T(8,128)(2,1)S(1)}, u32[]{:S(2)}, u32[]{:S(2)}) collective-permute-start(bf16[64,1,8,128]{3,0,2,1:T(8,128)(2,1)} %get-tuple-element.29), channel_id=1, source_target_pairs={{0,8},{8,16},{16,24},{24,32},{32,40},{40,48},{48,56},{56,64},{64,7... | collective-permute-start | bytes 393224 | tf_op jit(solution)/shard_map/ppermute | solution.py:18
  22.3 12.8 %collective-permute-start.5 = (bf16[64,1,8,128]{3,0,2,1:T(8,128)(2,1)}, bf16[64,1,8,128]{3,0,2,1:T(8,128)(2,1)}, u32[]{:S(2)}, u32[]{:S(2)}) collective-permute-start(bf16[64,1,8,128]{3,0,2,1:T(8,128)(2,1)} %get-tuple-element.30), channel_id=1, source_target_pairs={{8,0},{16,8},{24,16},{32,24},{40,32},{48,40},{56,48},{64,56},{72,6... | collective-permute-start | bytes 393224 | tf_op jit(solution)/shard_map/ppermute | solution.py:20
  24.2 8.4 %copy-start.14 = (bf16[128]{0:T(256)(128)(2,1)S(1)}, bf16[128]{0:T(256)(128)(2,1)}, u32[]{:S(2)}) copy-start(bf16[128]{0:T(256)(128)(2,1)} %copy-done.13) | copy-start | bytes 772
  24.3 7.0 %copy-start.5 = (bf16[64,1,8,128]{3,0,2,1:T(8,128)(2,1)}, bf16[64,1,8,128]{3,0,2,1:T(8,128)(2,1)S(1)}, u32[]{:S(2)}) copy-start(bf16[64,1,8,128]{3,0,2,1:T(8,128)(2,1)S(1)} %collective-permute-done) | copy-start | bytes 393220
  24.3 6.9 %copy-start.7 = (bf16[64,1,8,128]{3,0,2,1:T(8,128)(2,1)}, bf16[64,1,8,128]{3,0,2,1:T(8,128)(2,1)S(1)}, u32[]{:S(2)}) copy-start(bf16[64,1,8,128]{3,0,2,1:T(8,128)(2,1)S(1)} %collective-permute-done.1) | copy-start | bytes 393220
  25.1 18.0 %collective-permute-start.2 = (bf16[64,10,1,128]{3,0,2,1:T(8,128)(2,1)}, bf16[64,10,1,128]{3,0,2,1:T(8,128)(2,1)}, u32[]{:S(2)}, u32[]{:S(2)}) collective-permute-start(bf16[64,10,1,128]{3,0,2,1:T(8,128)(2,1)} %get-tuple-element.25), channel_id=1, source_target_pairs={{0,1},{1,2},{2,3},{3,4},{4,5},{5,6},{6,7},{8,9},{9,10},{10,11},{11... | collective-permute-start | bytes 491528 | tf_op jit(solution)/shard_map/ppermute | solution.py:18
  31.2 11.9 %collective-permute-start.3 = (bf16[64,10,1,128]{3,0,2,1:T(8,128)(2,1)}, bf16[64,10,1,128]{3,0,2,1:T(8,128)(2,1)}, u32[]{:S(2)}, u32[]{:S(2)}) collective-permute-start(bf16[64,10,1,128]{3,0,2,1:T(8,128)(2,1)} %get-tuple-element.26), channel_id=1, source_target_pairs={{1,0},{2,1},{3,2},{4,3},{5,4},{6,5},{7,6},{9,8},{10,9},{11,10},{12... | collective-permute-start | bytes 491528 | tf_op jit(solution)/shard_map/ppermute | solution.py:20
  35.8 23.1 %collective-permute-start.6 = (bf16[64,10,1,128]{3,0,2,1:T(8,128)(2,1)S(1)}, bf16[64,10,1,128]{3,0,2,1:T(8,128)(2,1)S(1)}, u32[]{:S(2)}, u32[]{:S(2)}) collective-permute-start(bf16[64,10,1,128]{3,0,2,1:T(8,128)(2,1)S(1)} %get-tuple-element.23), channel_id=1, source_target_pairs={{0,1},{1,2},{2,3},{3,4},{4,5},{5,6},{6,7},{8,9},{9,10},{10,11},{11... | collective-permute-start | bytes 491528 | tf_op jit(solution)/shard_map/ppermute | solution.py:18
  41.3 17.6 %collective-permute-start.7 = (bf16[64,10,1,128]{3,0,2,1:T(8,128)(2,1)S(1)}, bf16[64,10,1,128]{3,0,2,1:T(8,128)(2,1)S(1)}, u32[]{:S(2)}, u32[]{:S(2)}) collective-permute-start(bf16[64,10,1,128]{3,0,2,1:T(8,128)(2,1)S(1)} %get-tuple-element.24), channel_id=1, source_target_pairs={{1,0},{2,1},{3,2},{4,3},{5,4},{6,5},{7,6},{9,8},{10,9},{11,10},{12... | collective-permute-start | bytes 491528 | tf_op jit(solution)/shard_map/ppermute | solution.py:20
  47.1 0.9 copy-start.6
  47.2 1.0 copy-start.8
  62.9 2.1 copy-start.11
  80.0 1.6 copy-start.4
  92.4 1.2 copy-start.10
  93.6 15.4 %collective-permute-start.8 = (bf16[64,1,8,128]{3,0,2,1:T(8,128)(2,1)S(1)}, bf16[64,1,8,128]{3,0,2,1:T(8,128)(2,1)S(1)}, u32[]{:S(2)}, u32[]{:S(2)}) collective-permute-start(bf16[64,1,8,128]{3,0,2,1:T(8,128)(2,1)S(1)} %get-tuple-element.27), channel_id=1, source_target_pairs={{0,8},{8,16},{16,24},{24,32},{32,40},{40,48},{48,56},{56,64},{64,7... | collective-permute-start | bytes 393224 | tf_op jit(solution)/shard_map/ppermute | solution.py:18
  98.0 10.9 %collective-permute-start.9 = (bf16[64,1,8,128]{3,0,2,1:T(8,128)(2,1)S(1)}, bf16[64,1,8,128]{3,0,2,1:T(8,128)(2,1)S(1)}, u32[]{:S(2)}, u32[]{:S(2)}) collective-permute-start(bf16[64,1,8,128]{3,0,2,1:T(8,128)(2,1)S(1)} %get-tuple-element.28), channel_id=1, source_target_pairs={{8,0},{16,8},{24,16},{32,24},{40,32},{48,40},{56,48},{64,56},{72,6... | collective-permute-start | bytes 393224 | tf_op jit(solution)/shard_map/ppermute | solution.py:20
  109.0 9.8 %collective-permute-start.10 = (bf16[64,10,1,128]{3,0,2,1:T(8,128)(2,1)S(1)}, bf16[64,10,1,128]{3,0,2,1:T(8,128)(2,1)S(1)}, u32[]{:S(2)}, u32[]{:S(2)}) collective-permute-start(bf16[64,10,1,128]{3,0,2,1:T(8,128)(2,1)S(1)} %get-tuple-element.21), channel_id=1, source_target_pairs={{0,1},{1,2},{2,3},{3,4},{4,5},{5,6},{6,7},{8,9},{9,10},{10,11},{11... | collective-permute-start | bytes 491528 | tf_op jit(solution)/shard_map/ppermute | solution.py:18
  114.8 7.6 %collective-permute-start.11 = (bf16[64,10,1,128]{3,0,2,1:T(8,128)(2,1)S(1)}, bf16[64,10,1,128]{3,0,2,1:T(8,128)(2,1)S(1)}, u32[]{:S(2)}, u32[]{:S(2)}) collective-permute-start(bf16[64,10,1,128]{3,0,2,1:T(8,128)(2,1)S(1)} %get-tuple-element.22), channel_id=1, source_target_pairs={{1,0},{2,1},{3,2},{4,3},{5,4},{6,5},{7,6},{9,8},{10,9},{11,10},{12... | collective-permute-start | bytes 491528 | tf_op jit(solution)/shard_map/ppermute | solution.py:20
  118.6 233.7 %all-reduce.8.cloned.1.call-start = ((), (), s32[]{:S(2)}) async-start(), calls=%async_computation | async-start | bytes 3538944 | tf_op jit(solution)/shard_map/psum | solution.py:125
  126.4 4.4 %copy-start.3 = (bf16[3,3,3,64,64]{4,3,2,1,0:T(8,128)(2,1)S(1)}, bf16[3,3,3,64,64]{4,3,2,1,0:T(8,128)(2,1)}, u32[]{:S(2)}) copy-start(bf16[3,3,3,64,64]{4,3,2,1,0:T(8,128)(2,1)} %copy.39) | copy-start | bytes 663556
  130.8 13.3 %copy-start = (bf16[192,10,10,128]{3,0,2,1:T(8,128)(2,1)}, bf16[192,10,10,128]{3,0,2,1:T(8,128)(2,1)S(1)}, u32[]{:S(2)}) copy-start(bf16[192,10,10,128]{3,0,2,1:T(8,128)(2,1)S(1)} %pad_maximum_fusion.3) | copy-start | bytes 14745604
  144.1 80.7 %copy-start.1 = (bf16[64,8,8,128]{3,2,1,0:T(8,128)(2,1)S(1)}, bf16[64,8,8,128]{3,2,1,0:T(8,128)(2,1)}, u32[]{:S(2)}) copy-start(bf16[64,8,8,128]{3,2,1,0:T(8,128)(2,1)} %param.6) | copy-start | bytes 3145732
  144.1 80.7 %copy-start.12 = (f32[128]{0:T(128)S(1)}, f32[128]{0:T(128)}, u32[]{:S(2)}) copy-start(f32[128]{0:T(128)} %convert_element_type.41) | copy-start | bytes 1540
Sparse Core Ops, SparseCore 0:
  118.7 105.8 all-reduce.9
  227.3 124.9 all-reduce.7
